TPU v7x, 32 devices: a whole 2x2x4 slice. The times are simulated.
32 devices in a mesh: swap: 2 (over core), ep: 16 (over z, y, x).
Axes of the slice: x: 2, y: 2, z: 4, core: 2. Of those that a mesh axis runs over, the one named last changes fastest.
Arguments:
- grad_out: bfloat16 [2048, 6144], P('ep'), may hold values from -6 to 6
- parked_inputs: bfloat16 [2, 2048, 3072], P('swap', 'ep'), may hold values from -6 to 6
- route_ids: int32 [2048, 2], P('ep'), may hold values from 0 to 7, all different within a row; in each aligned block of 128 rows (0 to 127, 128 to 255, ...) at most 34 rows name the same one
- route_probs: float32 [2048, 2], P('ep'), may hold values from 0.1 to 0.9
- flight_expert: int32 [1], replicated, may hold values from 0 to 7
- w_gate: bfloat16 [6144, 8192], P(None, 'ep'), may hold values from -0.078125 to 0.078125
- w_up: bfloat16 [6144, 8192], P(None, 'ep'), may hold values from -0.078125 to 0.078125
- w_down: bfloat16 [8192, 6144], P('ep'), may hold values from -0.0625 to 0.0625
Outputs:
- grad_in: bfloat16 [2048, 6144], P('ep', 'swap')
Inputs may be any that keep to these rules, and one draw needn't show every extreme that they name: `route_ids`: each row names 2 different experts; the rows of one device name any one expert at most 34 times.
All inputs are finite; a program needn't handle non-finite values.
Results may differ from a plain program's by a relative error of at most 0.0024.
Values may be sent and summed in bfloat16 or wider, within the bound.
No kernel may reach another device: no remote copies, remote signals or barrier semaphores. Data moves between devices by JAX's collectives and lax.ppermute only.
A program may use at most 256 MiB of HBM per device.

v0:
```python
import jax
import jax.numpy as jnp
from jax import lax
from jax.sharding import PartitionSpec as P

CAP = 34


def partner_2(value, axis, apart):
    mask = 2**apart
    pairs = [(source, source ^ mask) for source in range(lax.axis_size(axis))]
    return lax.ppermute(value, axis, pairs)


def join_by_bit(mine, other, upper, axis):
    low_first = jnp.concatenate([mine, other], axis=axis)
    high_first = jnp.concatenate([other, mine], axis=axis)
    return jnp.where(upper == 1, high_first, low_first)


def on_device(grad_out, parked_inputs, route_ids, route_probs, flight_expert, w_gate, w_up, w_down):
    tokens_here = grad_out.shape[0]
    features = grad_out.shape[1]
    feat_half = features // 2
    half_cap = CAP // 2
    core = lax.axis_index("swap")
    ep_place = lax.axis_index("ep")
    hits = route_ids == flight_expert[0]
    weight = jnp.sum(jnp.where(hits, route_probs, jnp.float32(0.0)), axis=1)
    flags = jnp.any(hits, axis=1).astype(jnp.int32)
    ranks = jnp.cumsum(flags) - flags
    slot_ids = jnp.arange(CAP, dtype=jnp.int32)
    match = (ranks[None, :] == slot_ids[:, None]) & (flags[None, :] == 1)
    token_ids = jnp.arange(tokens_here, dtype=jnp.int32)
    slot_tok = jnp.sum(jnp.where(match, token_ids[None, :], 0), axis=1)
    valid = jnp.any(match, axis=1)
    mine_tok = lax.dynamic_slice_in_dim(slot_tok, core * half_cap, half_cap)
    mine_valid = lax.dynamic_slice_in_dim(valid, core * half_cap, half_cap)
    own_half = parked_inputs[0]
    partner = partner_2(own_half, "swap", 0)
    full_inputs = join_by_bit(own_half, partner, core, 1)
    x_rows = jnp.take(full_inputs, mine_tok, axis=0)
    zero = jnp.zeros((), jnp.bfloat16)
    x_rows = jnp.where(mine_valid[:, None], x_rows, zero)
    dy_rows = jnp.where(mine_valid[:, None], jnp.take(grad_out, mine_tok, axis=0), zero)
    nbits = lax.axis_size("ep").bit_length() - 1
    row_bits = list(range(3, nbits))
    col_bits = [0, 1, 2]
    rows_pair = (dy_rows[None], x_rows[None])
    for bit in row_bits:
        upper = ep_place // (1 << bit) % 2
        arrived = partner_2((rows_pair[0], rows_pair[1]), "ep", bit)
        rows_pair = (
            join_by_bit(rows_pair[0], arrived[0], upper, 0),
            join_by_bit(rows_pair[1], arrived[1], upper, 0),
        )
    gate_cols, up_cols, down_rows = (w_gate, w_up, w_down)
    for bit in col_bits:
        upper = ep_place // (1 << bit) % 2
        arrived = partner_2((gate_cols, up_cols, down_rows), "ep", bit)
        gate_cols = join_by_bit(gate_cols, arrived[0], upper, 1)
        up_cols = join_by_bit(up_cols, arrived[1], upper, 1)
        down_rows = join_by_bit(down_rows, arrived[2], upper, 0)
    dy_all = rows_pair[0].reshape(-1, features)
    x_all = rows_pair[1].reshape(-1, features)
    contract = (((1,), (1,)), ((), ()))
    gate = jnp.dot(x_all, gate_cols, preferred_element_type=jnp.float32)
    up = jnp.dot(x_all, up_cols, preferred_element_type=jnp.float32)
    dhid = lax.dot_general(dy_all, down_rows, contract, preferred_element_type=jnp.float32)
    sig = jax.nn.sigmoid(gate)
    d_up = (dhid * gate * sig).astype(jnp.bfloat16)
    d_gate = (dhid * up * sig * (1.0 + gate * (1.0 - sig))).astype(jnp.bfloat16)
    partial_value = lax.dot_general(d_gate, gate_cols, contract, preferred_element_type=jnp.float32)
    partial_value = partial_value + lax.dot_general(
        d_up, up_cols, contract, preferred_element_type=jnp.float32
    )
    partial_value = partial_value.reshape(-1, half_cap, features)
    for bit in reversed(row_bits):
        upper = ep_place // (1 << bit) % 2
        middle = partial_value.shape[0] // 2
        lower_part = partial_value[:middle]
        upper_part = partial_value[middle:]
        keeping = jnp.where(upper == 1, upper_part, lower_part)
        sending = jnp.where(upper == 1, lower_part, upper_part)
        partial_value = keeping + partner_2(sending.astype(jnp.bfloat16), "ep", bit).astype(
            sending.dtype
        )
    mine_sum = partial_value[0]
    keep_cols = lax.dynamic_slice_in_dim(mine_sum, core * feat_half, feat_half, 1)
    send_cols = lax.dynamic_slice_in_dim(mine_sum, (1 - core) * feat_half, feat_half, 1)
    theirs = partner_2(send_cols.astype(jnp.bfloat16), "swap", 0).astype(send_cols.dtype)
    slot_rows = join_by_bit(keep_cols, theirs, core, 0)
    contrib = jnp.einsum(
        "ct,cd->td", match.astype(jnp.float32), slot_rows, precision=lax.Precision.HIGHEST
    )
    own_grad = lax.dynamic_slice_in_dim(grad_out, core * feat_half, feat_half, 1)
    total = own_grad.astype(jnp.float32) + 0.5 * weight[:, None] * contrib
    return total.astype(jnp.bfloat16)


def solution(mesh):
    in_specs = (
        P("ep", None),
        P("swap", "ep", None),
        P("ep", None),
        P("ep", None),
        P(),
        P(None, "ep"),
        P(None, "ep"),
        P("ep", None),
    )
    out_specs = P("ep", "swap")
    return jax.shard_map(
        on_device, mesh=mesh, in_specs=in_specs, out_specs=out_specs, check_vma=False
    )
```

profile of v0, /device:TPU:0, one launch (start us, length us, event | category | flops | bytes accessed | tf_op | source)
XLA Modules:
  0.0 2298.9 jit_solution(8454392270870823050)
XLA Ops:
  0.0 3.0 collective-permute-start.1
  3.0 136.6 %collective-permute-done.1 = bf16[512,6144]{1,0:T(8,128)(2,1)} collective-permute-done((bf16[512,6144]{1,0:T(8,128)(2,1)}, bf16[512,6144]{1,0:T(8,128)(2,1)}, u32[]{:S(2)}, u32[]{:S(2)}) %collective-permute-start.1) | collective-permute-done | bytes 6291488 | tf_op jit(solution)/shard_map/ppermute | solution.py:12
  139.6 15.8 maximum_select_fusion.7
  155.4 2.1 collective-permute-start.2
  157.5 1.5 collective-permute-start.6
  159.0 115.5 %collective-permute-done.9 = bf16[6144,512]{1,0:T(8,128)(2,1)} collective-permute-done((bf16[6144,512]{1,0:T(8,128)(2,1)}, bf16[6144,512]{1,0:T(8,128)(2,1)}, u32[]{:S(2)}, u32[]{:S(2)}) %collective-permute-start.9) | collective-permute-done | bytes 6291488 | tf_op jit(solution)/shard_map/ppermute | solution.py:12
  274.5 12.6 maximum_select_fusion.9
  287.0 2.1 collective-permute-start.10
  289.1 119.4 %collective-permute-done.6 = bf16[6144,512]{1,0:T(8,128)(2,1)} collective-permute-done((bf16[6144,512]{1,0:T(8,128)(2,1)}, bf16[6144,512]{1,0:T(8,128)(2,1)}, u32[]{:S(2)}, u32[]{:S(2)}) %collective-permute-start.6) | collective-permute-done | bytes 6291488 | tf_op jit(solution)/shard_map/ppermute | solution.py:12
  408.4 16.0 maximum_select_fusion.8
  424.4 1.8 collective-permute-start.7
  426.2 2.7 collective-permute-done.2
  429.0 26.2 %maximum_select_fusion.4 = bf16[2048,6144]{1,0:T(8,128)(2,1)} fusion(bf16[1024,6144]{1,0:T(8,128)(2,1)} %maximum_select_fusion.7, bf16[1024,6144]{1,0:T(8,128)(2,1)} %collective-permute-done.2, pred[]{:T(512)S(6)} %eq.71), kind=kLoop, calls=%fused_computation.12 | loop fusion | flops 113246208 | bytes 50331648 | tf_op jit(solution)/shard_map/jit(_where)/select_n | solution.py:18
  455.2 2.1 collective-permute-start.3
  457.3 241.3 %collective-permute-done.10 = bf16[6144,1024]{1,0:T(8,128)(2,1)} collective-permute-done((bf16[6144,1024]{1,0:T(8,128)(2,1)}, bf16[6144,1024]{1,0:T(8,128)(2,1)}, u32[]{:S(2)}, u32[]{:S(2)}) %collective-permute-start.10) | collective-permute-done | bytes 12582944 | tf_op jit(solution)/shard_map/ppermute | solution.py:12
  698.6 26.1 %maximum_select_fusion.6 = bf16[6144,2048]{1,0:T(8,128)(2,1)} fusion(bf16[6144,1024]{1,0:T(8,128)(2,1)} %maximum_select_fusion.9, bf16[6144,1024]{1,0:T(8,128)(2,1)} %collective-permute-done.10, pred[]{:T(512)S(6)} %eq.71), kind=kLoop, calls=%fused_computation.14 | loop fusion | flops 113246208 | bytes 50331648 | tf_op jit(solution)/shard_map/jit(_where)/select_n | solution.py:18
  724.8 2.1 collective-permute-start.11
  726.9 238.7 %collective-permute-done.7 = bf16[6144,1024]{1,0:T(8,128)(2,1)} collective-permute-done((bf16[6144,1024]{1,0:T(8,128)(2,1)}, bf16[6144,1024]{1,0:T(8,128)(2,1)}, u32[]{:S(2)}, u32[]{:S(2)}) %collective-permute-start.7) | collective-permute-done | bytes 12582944 | tf_op jit(solution)/shard_map/ppermute | solution.py:12
  965.7 26.0 %maximum_select_fusion.5 = bf16[6144,2048]{1,0:T(8,128)(2,1)} fusion(bf16[6144,1024]{1,0:T(8,128)(2,1)} %maximum_select_fusion.8, bf16[6144,1024]{1,0:T(8,128)(2,1)} %collective-permute-done.7, pred[]{:T(512)S(6)} %eq.71), kind=kLoop, calls=%fused_computation.13 | loop fusion | flops 113246208 | bytes 50331648 | tf_op jit(solution)/shard_map/jit(_where)/select_n | solution.py:18
  991.7 1.6 collective-permute-start.8
  994.0 0.1 copy.11
  994.1 0.2 reduce-window.8
  994.3 0.1 reduce
  994.4 0.1 fusion.31
  994.6 0.3 copy-done.8
  994.9 0.1 select_reduce_fusion
  995.2 0.7 gather_fusion
  995.9 0.4 maximum_select_fusion.24
  996.3 0.7 gather_fusion.1
  996.9 0.1 fusion.25
  997.1 2.7 collective-permute-start.5
  999.7 0.5 select_reduce_fusion.1
  1000.3 0.3 collective-permute-start
  1000.6 1079.9 %collective-permute-done.5 = bf16[1,17,6144]{2,1,0:T(8,128)(2,1)S(1)} collective-permute-done((bf16[1,17,6144]{2,1,0:T(8,128)(2,1)S(1)}, bf16[1,17,6144]{2,1,0:T(8,128)(2,1)S(1)}, u32[]{:S(2)}, u32[]{:S(2)}) %collective-permute-start.5) | collective-permute-done | bytes 208928 | tf_op jit(solution)/shard_map/ppermute | solution.py:12
  2080.5 0.1 maximum_select_fusion.26
  2080.6 0.1 select_n.205
  2080.8 2.9 collective-permute-done
  2083.7 0.1 maximum_select_fusion.25
  2083.8 0.1 select_n.189
  2083.9 32.6 %fusion = f32[34,4096]{1,0:T(8,128)S(1)} fusion(bf16[34,6144]{1,0:T(8,128)(2,1)S(1)} %select_n.189, bf16[2048,6144]{1,0:T(8,128)(2,1)} %maximum_select_fusion.4, bf16[2048,6144]{1,0:T(8,128)(2,1)} %collective-permute-done.3, pred[]{:T(512)S(6)} %eq.70), kind=kOutput, calls=%fused_computation.3 | convolution fusion | flops 1937768448 | bytes 51306496 | tf_op jit(solution)/shard_map/dot_general | solution.py:69
  2116.5 40.5 %fusion.8 = f32[34,4096]{1,0:T(8,128)S(1)} fusion(bf16[34,6144]{1,0:T(8,128)(2,1)S(1)} %select_n.205, bf16[6144,2048]{1,0:T(8,128)(2,1)} %maximum_select_fusion.6, bf16[6144,2048]{1,0:T(8,128)(2,1)} %collective-permute-done.11, pred[]{:T(512)S(6)} %eq.70), kind=kOutput, calls=%fused_computation.19 | convolution fusion | flops 1937768448 | bytes 51306496 | tf_op jit(solution)/shard_map/dot_general | solution.py:67
  2157.0 41.9 %fusion.15 = bf16[34,4096]{1,0:T(8,128)(2,1)} fusion(f32[34,4096]{1,0:T(8,128)S(1)} %fusion, bf16[34,6144]{1,0:T(8,128)(2,1)S(1)} %select_n.205, bf16[6144,2048]{1,0:T(8,128)(2,1)} %maximum_select_fusion.5, bf16[6144,2048]{1,0:T(8,128)(2,1)} %collective-permute-done.8, pred[]{:T(512)S(6)} %eq.70, f32[34,4096]{1,0:T(8,128)S(1)} %fusion.8), kind=kOutput, calls=%fused_computation.26 | convolution fusion | flops 1939161088 | bytes 52142080 | tf_op jit(solution)/shard_map/dot_general | solution.py:68
  2198.9 43.1 %fusion.9 = f32[34,6144]{1,0:T(8,128)S(1)} fusion(bf16[6144,2048]{1,0:T(8,128)(2,1)} %maximum_select_fusion.5, bf16[6144,2048]{1,0:T(8,128)(2,1)} %collective-permute-done.8, pred[]{:T(512)S(6)} %eq.70, f32[34,4096]{1,0:T(8,128)S(1)} %fusion, f32[34,4096]{1,0:T(8,128)S(1)} %fusion.8), kind=kOutput, calls=%fused_computation.20 | convolution fusion | flops 1938604032 | bytes 52281344 | tf_op jit(solution)/shard_map/dot_general | solution.py:74
  2242.0 41.8 %fusion.11 = f32[34,6144]{1,0:T(8,128)S(1)} fusion(f32[34,6144]{1,0:T(8,128)S(1)} %fusion.9, bf16[34,4096]{1,0:T(8,128)(2,1)} %fusion.15, bf16[6144,2048]{1,0:T(8,128)(2,1)} %maximum_select_fusion.6, bf16[6144,2048]{1,0:T(8,128)(2,1)} %collective-permute-done.11, pred[]{:T(512)S(6)} %eq.70), kind=kOutput, calls=%fused_computation.22 | convolution fusion | flops 1937977344 | bytes 52281344 | tf_op jit(solution)/shard_map/dot_general | solution.py:73
  2284.0 3.4 collective-permute-start.12
  2287.4 8.1 collective-permute-done.12
  2295.8 1.3 collective-permute-done.13
  2297.1 1.8 fusion.17
  (43 shorter events, 0.7 us)
Async XLA Ops:
  0.0 274.5 %slice-start = ((s8[6291456]{0:T(1024)(128)(4,1)}), s8[2097152]{0:T(1024)(128)(4,1)S(1)}, s32[]{:S(2)}) async-start(s8[6291456]{0:T(1024)(128)(4,1)} %bitcast.22), calls=%async_computation | async-start | bytes 4194304
  0.0 139.6 %collective-permute-start.1 = (bf16[512,6144]{1,0:T(8,128)(2,1)}, bf16[512,6144]{1,0:T(8,128)(2,1)}, u32[]{:S(2)}, u32[]{:S(2)}) collective-permute-start(bf16[512,6144]{1,0:T(8,128)(2,1)} %param.17), channel_id=1, source_target_pairs={{0,1},{1,0},{2,3},{3,2},{4,5},{5,4},{6,7},{7,6},{8,9},{9,8},{10,11... | collective-permute-start | bytes 18874376 | tf_op jit(solution)/shard_map/ppermute | solution.py:12
  3.0 271.5 %collective-permute-start.9 = (bf16[6144,512]{1,0:T(8,128)(2,1)}, bf16[6144,512]{1,0:T(8,128)(2,1)}, u32[]{:S(2)}, u32[]{:S(2)}) collective-permute-start(bf16[6144,512]{1,0:T(8,128)(2,1)} %param.15), channel_id=1, source_target_pairs={{0,1},{1,0},{2,3},{3,2},{4,5},{5,4},{6,7},{7,6},{8,9},{9,8},{10,11... | collective-permute-start | bytes 18874376 | tf_op jit(solution)/shard_map/ppermute | solution.py:12
  3.0 271.4 %slice-start.1 = ((s8[6291456]{0:T(1024)(128)(4,1)}), s8[4194304]{0:T(1024)(128)(4,1)S(1)}, s32[]{:S(2)}) async-start(s8[6291456]{0:T(1024)(128)(4,1)} %bitcast.22), calls=%async_computation.1 | async-start | bytes 8388608
  155.4 273.6 %collective-permute-start.2 = (bf16[1024,6144]{1,0:T(8,128)(2,1)}, bf16[1024,6144]{1,0:T(8,128)(2,1)}, u32[]{:S(2)}, u32[]{:S(2)}) collective-permute-start(bf16[1024,6144]{1,0:T(8,128)(2,1)} %maximum_select_fusion.7), channel_id=1, source_target_pairs={{0,2},{1,3},{2,0},{3,1},{4,6},{5,7},{6,4},{7,5},{8,10},{9,11},{10,... | collective-permute-start | bytes 37748744 | tf_op jit(solution)/shard_map/ppermute | solution.py:12
  157.5 251.0 %collective-permute-start.6 = (bf16[6144,512]{1,0:T(8,128)(2,1)}, bf16[6144,512]{1,0:T(8,128)(2,1)}, u32[]{:S(2)}, u32[]{:S(2)}) collective-permute-start(bf16[6144,512]{1,0:T(8,128)(2,1)} %param.16), channel_id=1, source_target_pairs={{0,1},{1,0},{2,3},{3,2},{4,5},{5,4},{6,7},{7,6},{8,9},{9,8},{10,11... | collective-permute-start | bytes 18874376 | tf_op jit(solution)/shard_map/ppermute | solution.py:12
  287.0 411.6 %collective-permute-start.10 = (bf16[6144,1024]{1,0:T(8,128)(2,1)}, bf16[6144,1024]{1,0:T(8,128)(2,1)}, u32[]{:S(2)}, u32[]{:S(2)}) collective-permute-start(bf16[6144,1024]{1,0:T(8,128)(2,1)} %maximum_select_fusion.9), channel_id=1, source_target_pairs={{0,2},{1,3},{2,0},{3,1},{4,6},{5,7},{6,4},{7,5},{8,10},{9,11},{10,... | collective-permute-start | bytes 37748744 | tf_op jit(solution)/shard_map/ppermute | solution.py:12
  424.4 541.2 %collective-permute-start.7 = (bf16[6144,1024]{1,0:T(8,128)(2,1)}, bf16[6144,1024]{1,0:T(8,128)(2,1)}, u32[]{:S(2)}, u32[]{:S(2)}) collective-permute-start(bf16[6144,1024]{1,0:T(8,128)(2,1)} %maximum_select_fusion.8), channel_id=1, source_target_pairs={{0,2},{1,3},{2,0},{3,1},{4,6},{5,7},{6,4},{7,5},{8,10},{9,11},{10,... | collective-permute-start | bytes 37748744 | tf_op jit(solution)/shard_map/ppermute | solution.py:12
  455.2 1628.7 %collective-permute-start.3 = (bf16[2048,6144]{1,0:T(8,128)(2,1)}, bf16[2048,6144]{1,0:T(8,128)(2,1)}, u32[]{:S(2)}, u32[]{:S(2)}) collective-permute-start(bf16[2048,6144]{1,0:T(8,128)(2,1)} %maximum_select_fusion.4), channel_id=1, source_target_pairs={{0,4},{1,5},{2,6},{3,7},{4,0},{5,1},{6,2},{7,3},{8,12},{9,13},{10,... | collective-permute-start | bytes 75497480 | tf_op jit(solution)/shard_map/ppermute | solution.py:12
  724.7 268.5 %copy-start.2 = (bf16[1,128,3072]{2,1,0:T(8,128)(2,1)S(1)}, bf16[1,128,3072]{2,1,0:T(8,128)(2,1)}, u32[]{:S(2)}) copy-start(bf16[1,128,3072]{2,1,0:T(8,128)(2,1)} %param.11) | copy-start | bytes 2359300
  724.8 269.2 %copy-start.3 = (s32[128,2]{0,1:T(2,128)S(1)}, s32[128,2]{0,1:T(2,128)}, u32[]{:S(2)}) copy-start(s32[128,2]{0,1:T(2,128)} %param.12) | copy-start | bytes 3076
  724.8 270.4 %copy-start = (bf16[128,6144]{1,0:T(8,128)(2,1)S(1)}, bf16[128,6144]{1,0:T(8,128)(2,1)}, u32[]{:S(2)}) copy-start(bf16[128,6144]{1,0:T(8,128)(2,1)} %param.10) | copy-start | bytes 4718596
  724.8 275.0 %copy-start.4 = (f32[128,2]{0,1:T(2,128)S(1)}, f32[128,2]{0,1:T(2,128)}, u32[]{:S(2)}) copy-start(f32[128,2]{0,1:T(2,128)} %param.13) | copy-start | bytes 3076
  724.8 1391.7 %collective-permute-start.11 = (bf16[6144,2048]{1,0:T(8,128)(2,1)}, bf16[6144,2048]{1,0:T(8,128)(2,1)}, u32[]{:S(2)}, u32[]{:S(2)}) collective-permute-start(bf16[6144,2048]{1,0:T(8,128)(2,1)} %maximum_select_fusion.6), channel_id=1, source_target_pairs={{0,4},{1,5},{2,6},{3,7},{4,0},{5,1},{6,2},{7,3},{8,12},{9,13},{10,... | collective-permute-start | bytes 75497480 | tf_op jit(solution)/shard_map/ppermute | solution.py:12
  991.7 1165.3 %collective-permute-start.8 = (bf16[6144,2048]{1,0:T(8,128)(2,1)}, bf16[6144,2048]{1,0:T(8,128)(2,1)}, u32[]{:S(2)}, u32[]{:S(2)}) collective-permute-start(bf16[6144,2048]{1,0:T(8,128)(2,1)} %maximum_select_fusion.5), channel_id=1, source_target_pairs={{0,4},{1,5},{2,6},{3,7},{4,0},{5,1},{6,2},{7,3},{8,12},{9,13},{10,... | collective-permute-start | bytes 75497480 | tf_op jit(solution)/shard_map/ppermute | solution.py:12
  993.3 2.6 collective-permute-start.4
  994.0 1.2 copy-start.6
  994.4 0.5 copy-start.8
  997.1 1083.4 %collective-permute-start.5 = (bf16[1,17,6144]{2,1,0:T(8,128)(2,1)S(1)}, bf16[1,17,6144]{2,1,0:T(8,128)(2,1)S(1)}, u32[]{:S(2)}, u32[]{:S(2)}) collective-permute-start(bf16[1,17,6144]{2,1,0:T(8,128)(2,1)S(1)} %get-tuple-element.8), channel_id=1, source_target_pairs={{0,8},{1,9},{2,10},{3,11},{4,12},{5,13},{6,14},{7,15},{8,0},{9,1},... | collective-permute-start | bytes 626696 | tf_op jit(solution)/shard_map/ppermute | solution.py:12
  1000.3 1083.4 %collective-permute-start = (bf16[1,17,6144]{2,1,0:T(8,128)(2,1)S(1)}, bf16[1,17,6144]{2,1,0:T(8,128)(2,1)S(1)}, u32[]{:S(2)}, u32[]{:S(2)}) collective-permute-start(bf16[1,17,6144]{2,1,0:T(8,128)(2,1)S(1)} %get-tuple-element.9), channel_id=1, source_target_pairs={{0,8},{1,9},{2,10},{3,11},{4,12},{5,13},{6,14},{7,15},{8,0},{9,1},... | collective-permute-start | bytes 626696 | tf_op jit(solution)/shard_map/ppermute | solution.py:12
  2242.0 45.4 %copy-start.5 = (f32[128]{0:T(128)S(1)}, f32[128]{0:T(128)}, u32[]{:S(2)}) copy-start(f32[128]{0:T(128)} %select_reduce_fusion.1) | copy-start | bytes 1540
  2242.0 55.1 %copy-start.1 = (bf16[128,6144]{1,0:T(8,128)(2,1)S(1)}, bf16[128,6144]{1,0:T(8,128)(2,1)}, u32[]{:S(2)}) copy-start(bf16[128,6144]{1,0:T(8,128)(2,1)} %param.10) | copy-start | bytes 4718596
  2242.0 55.1 %copy-start.7 = (pred[128]{0:T(512)(128)(4,1)S(1)}, pred[128]{0:T(512)(128)(4,1)}, u32[]{:S(2)}) copy-start(pred[128]{0:T(512)(128)(4,1)} %copy-done.6) | copy-start | bytes 388
  2242.0 55.1 %copy-start.9 = (s32[128]{0:T(128)S(1)}, s32[128]{0:T(128)}, u32[]{:S(2)}) copy-start(s32[128]{0:T(128)} %copy-done.8) | copy-start | bytes 1540
  2284.0 11.5 collective-permute-start.12
  2295.6 1.4 collective-permute-start.13
where the time goes:
time: 2300 us
  waiting for transfers between devices  1950 us (85%)
  matrix products  202 us (9%)
  other arithmetic  125 us (5%)
    ppermute x14, waiting for transfers between devices, partner_2(): return lax.ppermute(value, axis, pairs)  1950 us
    select_n x9, other arithmetic, join_by_bit(): return jnp.where(upper == 1, high_first, low_first)  123 us
  transfers between devices with their start and end apart: 14, of which 10 were waited for; matrix products, arithmetic and copies ran while one was open for 9% of the time, Pallas kernels for 0%

commit v1 on v0

v1 whole, which is shorter than its diff:
```python
import functools

import jax
import jax.numpy as jnp
from jax import lax
from jax.experimental import pallas as pl
from jax.experimental.pallas import tpu as pltpu
from jax.sharding import PartitionSpec as P


CAP = 34
PIECES = 4
RING = 4
KERNEL_VMEM = 24 << 20
f32 = jnp.float32
bf16 = jnp.bfloat16


def flip(value, bit):
    size = lax.axis_size("ep")
    return lax.ppermute(value, "ep", [(s, s ^ (1 << bit)) for s in range(size)])


def ring_next(value, ring):
    size = lax.axis_size("ep")
    span = 4 * ring
    pairs = []
    for s in range(size):
        base, inner = s // span * span, s % span
        pairs.append((s, base + (inner + 4) % span))
    return lax.ppermute(value, "ep", pairs)


VMEM_WHOLE = pl.BlockSpec(memory_space=pltpu.VMEM)
SMEM_WHOLE = pl.BlockSpec(memory_space=pltpu.SMEM)
HBM_WHOLE = pl.BlockSpec(memory_space=pltpu.HBM)


def in_hbm(*values):
    return [pltpu.with_memory_space_constraint(value, pltpu.HBM) for value in values]


def slots_of(fe_ref, ids_ref):
    hits = (ids_ref[...] == fe_ref[0]).astype(f32)
    flags = jnp.max(hits, axis=0, keepdims=True)
    tokens = flags.shape[1]
    row = lax.broadcasted_iota(jnp.int32, (tokens, tokens), 0)
    col = lax.broadcasted_iota(jnp.int32, (tokens, tokens), 1)
    before = (row < col).astype(bf16)
    ranks = jnp.dot(jnp.broadcast_to(flags, (16, tokens)).astype(bf16), before, preferred_element_type=f32)
    slot = lax.broadcasted_iota(jnp.int32, (CAP, tokens), 0).astype(f32)
    match = (ranks[:1] == slot) & (flags > 0.5)
    return match.astype(f32).astype(bf16), hits


def rows_body(core_ref, fe_ref, ids_ref, x_hbm, dy_hbm, out_ref, x_ref, dy_ref, sems):
    half = x_ref.shape[1]
    here = pl.ds(pl.multiple_of(core_ref[0] * half, 128), half)
    get_x = pltpu.make_async_copy(x_hbm.at[0], x_ref, sems.at[0])
    get_dy = pltpu.make_async_copy(dy_hbm.at[:, here], dy_ref, sems.at[1])
    get_x.start()
    get_dy.start()
    pick, _ = slots_of(fe_ref, ids_ref)
    width = out_ref.shape[1]
    for i, (copy, ref) in enumerate(((get_x, x_ref), (get_dy, dy_ref))):
        copy.wait()
        rows = jnp.dot(pick, ref[...], preferred_element_type=f32).astype(bf16)
        for q in range(PIECES):
            at = (i * PIECES + q) * CAP
            out_ref[at:at + CAP, :] = rows[:, q * width:(q + 1) * width]


def build_rows(core, flight_expert, ids, parked, grad_out):
    tokens, half = parked.shape[1:]
    width = half // PIECES
    return pl.pallas_call(
        rows_body,
        in_specs=[SMEM_WHOLE, SMEM_WHOLE, VMEM_WHOLE, HBM_WHOLE, HBM_WHOLE],
        out_specs=VMEM_WHOLE,
        out_shape=jax.ShapeDtypeStruct((2 * PIECES * CAP, width), bf16),
        scratch_shapes=[
            pltpu.VMEM((tokens, half), bf16),
            pltpu.VMEM((tokens, half), bf16),
            pltpu.SemaphoreType.DMA((2,)),
        ],
        compiler_params=pltpu.CompilerParams(vmem_limit_bytes=KERNEL_VMEM),
        name="rows",
    )(core, flight_expert, ids, *in_hbm(parked, grad_out))


def prep_body(core_ref, wg, wu, wd, og, ou, od, sems):
    half = og.shape[0]
    here = pl.ds(pl.multiple_of(core_ref[0] * half, 128), half)
    copies = (
        pltpu.make_async_copy(wg.at[here, :], og, sems.at[0]),
        pltpu.make_async_copy(wu.at[here, :], ou, sems.at[1]),
        pltpu.make_async_copy(wd.at[:, here], od, sems.at[2]),
    )
    for copy in copies:
        copy.start()
    for copy in copies:
        copy.wait()


def prep(core, w_gate, w_up, w_down):
    features, hidden = w_gate.shape
    half = features // 2
    return pl.pallas_call(
        prep_body,
        in_specs=[SMEM_WHOLE] + [HBM_WHOLE] * 3,
        out_specs=[VMEM_WHOLE] * 3,
        out_shape=[
            pltpu.VMEM((half, hidden), bf16),
            pltpu.VMEM((half, hidden), bf16),
            pltpu.VMEM((hidden, half), bf16),
        ],
        scratch_shapes=[pltpu.SemaphoreType.DMA((3,))],
        compiler_params=pltpu.CompilerParams(vmem_limit_bytes=KERNEL_VMEM),
        name="prep",
    )(core, *in_hbm(w_gate, w_up, w_down))


def first_body(plan, *refs):
    n = len(refs) - 5
    wg, wu, wd, out, out_low = refs[n:]
    width = refs[0].shape[1]
    total = None
    for q in range(PIECES):
        x = jnp.concatenate([refs[i][at + q * CAP:at + (q + 1) * CAP, :] for (i, at), _ in plan], axis=0)
        dy = jnp.concatenate([refs[i][at + q * CAP:at + (q + 1) * CAP, :] for _, (i, at) in plan], axis=0)
        here = slice(q * width, (q + 1) * width)
        g = jnp.dot(x, wg[here, :], preferred_element_type=f32)
        u = jnp.dot(x, wu[here, :], preferred_element_type=f32)
        h = lax.dot_general(dy, wd[:, here], (((1,), (1,)), ((), ())), preferred_element_type=f32)
        r = jnp.concatenate([g, u, h], axis=1)
        total = r if total is None else total + r
    out[...] = total
    out_low[...] = total.astype(bf16)


def first(arrays, plan, w_gate, w_up, w_down):
    hidden = w_gate.shape[1]
    rows = len(plan) * CAP
    return pl.pallas_call(
        functools.partial(first_body, plan),
        in_specs=[VMEM_WHOLE] * (len(arrays) + 3),
        out_specs=[VMEM_WHOLE] * 2,
        out_shape=[
            jax.ShapeDtypeStruct((rows, 3 * hidden), f32),
            jax.ShapeDtypeStruct((rows, 3 * hidden), bf16),
        ],
        compiler_params=pltpu.CompilerParams(vmem_limit_bytes=KERNEL_VMEM),
        name="first",
    )(*arrays, w_gate, w_up, w_down)


def second_body(mine_ref, theirs_ref, wg, wu, *outs):
    hidden = wg.shape[1]
    width = outs[0].shape[1]
    total = mine_ref[...] + theirs_ref[...].astype(f32)
    gate = total[:, :hidden]
    up = total[:, hidden:2 * hidden]
    dhid = total[:, 2 * hidden:]
    sig = jax.nn.sigmoid(gate)
    du = (dhid * gate * sig).astype(bf16)
    dg = (dhid * up * sig * (1.0 + gate * (1.0 - sig))).astype(bf16)
    dims = (((1,), (1,)), ((), ()))
    for q in range(PIECES):
        here = slice(q * width, (q + 1) * width)
        r = lax.dot_general(dg, wg[here, :], dims, preferred_element_type=f32)
        r = r + lax.dot_general(du, wu[here, :], dims, preferred_element_type=f32)
        r = r.astype(bf16)
        for i, out in enumerate(outs):
            out[q * CAP:(q + 1) * CAP, :] = r[i * CAP:(i + 1) * CAP, :]


def second(mine, theirs, w_gate, w_up, width):
    n = mine.shape[0] // CAP
    return pl.pallas_call(
        second_body,
        in_specs=[VMEM_WHOLE] * 4,
        out_specs=[VMEM_WHOLE] * n,
        out_shape=[jax.ShapeDtypeStruct((PIECES * CAP, width), bf16)] * n,
        compiler_params=pltpu.CompilerParams(vmem_limit_bytes=KERNEL_VMEM),
        name="second",
    )(mine, theirs, w_gate, w_up)


def last_body(core_ref, fe_ref, ids_ref, probs_ref, grad_hbm, p0_ref, sx_ref, sy_ref, sz_ref, out_ref, grad_ref, sem):
    half = grad_ref.shape[1]
    here = pl.ds(pl.multiple_of(core_ref[0] * half, 128), half)
    get = pltpu.make_async_copy(grad_hbm.at[:, here], grad_ref, sem)
    get.start()
    pick, hits = slots_of(fe_ref, ids_ref)
    weight = 0.5 * jnp.sum(hits * probs_ref[...], axis=0, keepdims=True)
    weight = jnp.broadcast_to(weight, (8, weight.shape[1])).T[:, :1]
    total = (p0_ref[...].astype(f32) + sx_ref[...].astype(f32)) + (sy_ref[...].astype(f32) + sz_ref[...].astype(f32))
    high = total.astype(bf16)
    low = (total - high.astype(f32)).astype(bf16)
    width = total.shape[1]
    dims = (((0,), (0,)), ((), ()))
    get.wait()
    for q in range(PIECES):
        at = slice(q * CAP, (q + 1) * CAP)
        contrib = lax.dot_general(pick, high[at], dims, preferred_element_type=f32)
        contrib = contrib + lax.dot_general(pick, low[at], dims, preferred_element_type=f32)
        here = slice(q * width, (q + 1) * width)
        out_ref[:, here] = (grad_ref[:, here].astype(f32) + weight * contrib).astype(bf16)


def finish(core, flight_expert, ids, probs, grad_out, parts):
    tokens = grad_out.shape[0]
    half = grad_out.shape[1] // 2
    return pl.pallas_call(
        last_body,
        in_specs=[SMEM_WHOLE, SMEM_WHOLE, VMEM_WHOLE, VMEM_WHOLE, HBM_WHOLE] + [VMEM_WHOLE] * len(parts),
        out_specs=VMEM_WHOLE,
        out_shape=jax.ShapeDtypeStruct((tokens, half), bf16),
        scratch_shapes=[pltpu.VMEM((tokens, half), bf16), pltpu.SemaphoreType.DMA],
        compiler_params=pltpu.CompilerParams(vmem_limit_bytes=KERNEL_VMEM),
        name="last",
    )(core, flight_expert, ids, probs, *in_hbm(grad_out), *parts)


def swap_cores(value):
    return lax.ppermute(value, "swap", [(0, 1), (1, 0)])


def on_device(grad_out, parked_inputs, route_ids, route_probs, flight_expert, w_gate, w_up, w_down):
    core = lax.axis_index("swap").reshape(1)
    size = lax.axis_size("ep")
    for bit in range((4 * RING).bit_length() - 1, size.bit_length() - 1):
        w_gate = jnp.concatenate([w_gate, flip(w_gate, bit)], axis=1)
        w_up = jnp.concatenate([w_up, flip(w_up, bit)], axis=1)
        w_down = jnp.concatenate([w_down, flip(w_down, bit)], axis=0)

    ids = route_ids.T

    def over_x(value):
        return flip(value, 0)

    def over_y(value):
        return flip(value, 1)

    def over_z(value):
        return ring_next(value, RING)

    own = build_rows(core, flight_expert, ids, parked_inputs, grad_out)
    w_gate, w_up, w_down = prep(core, w_gate, w_up, w_down)
    mid = own.shape[0] // 2
    width = own.shape[1]
    split = mid // 16 * 8

    chunk = [own]
    for _ in range(1, RING):
        chunk.append(over_z(chunk[-1]))
    from_x, parts = [None] * RING, [None] * RING
    for j in range(RING):
        if j == 2:
            fx = over_z(from_x[1])
            fy = over_y(chunk[2])
            arrays = (chunk[2], fx, fy, over_x(fy))
            plan = tuple(((i, 0), (i, mid)) for i in range(4))
        else:
            fx = over_x(chunk[j])
            fy = over_y(chunk[j])
            dl = over_y(fx[:mid])
            dh = over_x(fy[mid:])
            arrays = (chunk[j], fx, fy, dl, dh)
            plan = tuple(((i, 0), (i, mid)) for i in range(3)) + (((3, 0), (4, 0)),)
        from_x[j] = fx
        mine, low = first(arrays, plan, w_gate, w_up, w_down)
        theirs = swap_cores(low)
        parts[j] = second(mine, theirs, w_gate, w_up, width)

    def add(*values):
        total = values[0].astype(f32)
        for value in values[1:]:
            total = total + value.astype(f32)
        return total.astype(bf16)

    def low_rows(piece):
        return jnp.pad(piece.astype(f32), ((0, mid - split), (0, 0)))

    def high_rows(piece):
        return jnp.pad(piece.astype(f32), ((split, 0), (0, 0)))

    p0, px, py, pd = parts[1]
    py = add(py, over_x(pd))
    carry = over_z(add(p0, over_y(py)))
    carry_x = over_z(px)
    for j in list(range(2, RING)) + [0]:
        p0, px, py, pd = parts[j]
        low = over_y(pd[:split])
        px = add(px, low_rows(low), carry_x) if j == 2 else add(px, low_rows(low))
        py = add(py, high_rows(over_x(pd[split:])))
        sx = over_x(px)
        sy = over_y(py)
        if j > 0:
            carry = over_z(add(p0, sx, sy, carry))
    return finish(core, flight_expert, ids, route_probs.T, grad_out, (p0, sx, sy, carry))


def solution(mesh):
    in_specs = (
        P("ep", None),
        P("swap", "ep", None),
        P("ep", None),
        P("ep", None),
        P(),
        P(None, "ep"),
        P(None, "ep"),
        P("ep", None),
    )

    return jax.shard_map(on_device, mesh=mesh, in_specs=in_specs, out_specs=P("ep", "swap"), check_vma=False)
```

time: 2300 us -> 144 us (0.06)
  waiting for transfers between devices: 1950 us -> 76.7 us
  matrix products: 202 us -> 0 us
  other arithmetic: 125 us -> 0.56 us
  Pallas kernels: 0 us -> 25.4 us
    ppermute x14 -> x40, waiting for transfers between devices: 1950 us -> 76.7 us  [the longest x28 46.5 us: flip(): return lax.ppermute(value, 'ep', [(s, s ^ 1 << bit) for s in range(size)])]
    dot_general x6 -> x0, matrix products: 202 us -> none  [the longest x1 43.1 us: on_device(): lax.dot_general(d_up, up_cols, contract, preferred_element_type=jnp.float32)]
    select_n x9 -> x0, other arithmetic: 123 us -> none  [join_by_bit(): return jnp.where(upper == 1, high_first, low_first)]
    pallas_call x0 -> x11, Pallas kernels: none -> 25.4 us  [the longest x4 8.77 us: second(): pl.pallas_call(second_body, in_specs=[VMEM_WHOLE] * 4, out_specs=[VMEM_WH...]
  transfers between devices with their start and end apart: 14 -> 40, of which waited for: 10 -> 14; matrix products, arithmetic and copies ran while one was open for 9% -> 0% of each run, Pallas kernels for 0% -> 15%
where the time goes in v1:
time: 144 us
  waiting for transfers between devices  76.7 us (53%)
  starting transfers between devices  39.2 us (27%)
  Pallas kernels  25.4 us (18%)
    ppermute x28, waiting for transfers between devices, flip(): return lax.ppermute(value, 'ep', [(s, s ^ 1 << bit) for s in range(size)])  46.5 us
    ppermute x28, starting transfers between devices, flip(): return lax.ppermute(value, 'ep', [(s, s ^ 1 << bit) for s in range(size)])  31.6 us
    ppermute x8, waiting for transfers between devices, ring_next(): return lax.ppermute(value, 'ep', pairs)  30.3 us
    pallas_call x4, Pallas kernels, second(): pl.pallas_call(second_body, in_specs=[VMEM_WHOLE] * 4, out_specs=[VMEM_WH...  8.77 us
    pallas_call x4, Pallas kernels, first(): pl.pallas_call(functools.partial(first_body, plan), in_specs=[VMEM_WHOLE]...  8.58 us
    ppermute x8, starting transfers between devices, ring_next(): return lax.ppermute(value, 'ep', pairs)  7.27 us
    pallas_call x1, Pallas kernels, prep(): pl.pallas_call(prep_body, in_specs=[SMEM_WHOLE] + [HBM_WHOLE] * 3, out_sp...  3.78 us
  transfers between devices with their start and end apart: 40, of which 14 were waited for; matrix products, arithmetic and copies ran while one was open for 0% of the time, Pallas kernels for 15%

profile of v1, /device:TPU:0, one launch (start us, length us, event | category | flops | bytes accessed | tf_op | source)
XLA Modules:
  0.0 143.9 jit_solution(7681957596790104934)
XLA Ops:
  1.3 1.7 %rows.1.refs_0_ = bf16[272,768]{1,0:T(8,128)(2,1)S(1)} custom-call(s32[1]{0:T(128)} %bitcast.core_ref, s32[1]{0:T(128)S(6)} %copy.9.fe_ref, s32[2,128]{1,0:T(2,128)S(1)} %bitcast.3, bf16[1,128,3072]{2,1,0:T(8,128)(2,1)} %x_hbm.1, bf16[128,6144]{1,0:T(8,128)(2,1)} %grad_hbm.1), custom_call_target="tpu_custom_call" | custom-call | tf_op jit(solution)/shard_map/rows/pallas_call | solution.py:76
  3.0 3.1 %collective-permute-start.9 = (bf16[272,768]{1,0:T(8,128)(2,1)S(1)}, bf16[272,768]{1,0:T(8,128)(2,1)S(1)}, u32[]{:S(2)}, u32[]{:S(2)}) collective-permute-start(bf16[272,768]{1,0:T(8,128)(2,1)S(1)} %rows.1.refs_0_), channel_id=1, source_target_pairs={{0,4},{1,5},{2,6},{3,7},{4,8},{5,9},{6,10},{7,11},{8,12},{9,13},{1... | collective-permute-start | bytes 1253384 | tf_op jit(solution)/shard_map/ppermute | solution.py:31
  6.1 11.7 %collective-permute-done.9.refs_0_ = bf16[272,768]{1,0:T(8,128)(2,1)S(1)} collective-permute-done((bf16[272,768]{1,0:T(8,128)(2,1)S(1)}, bf16[272,768]{1,0:T(8,128)(2,1)S(1)}, u32[]{:S(2)}, u32[]{:S(2)}) %collective-permute-start.9) | collective-permute-done | bytes 417824 | tf_op jit(solution)/shard_map/ppermute | solution.py:31
  17.8 1.5 %collective-permute-start.21 = (bf16[272,768]{1,0:T(8,128)(2,1)S(1)}, bf16[272,768]{1,0:T(8,128)(2,1)S(1)}, u32[]{:S(2)}, u32[]{:S(2)}) collective-permute-start(bf16[272,768]{1,0:T(8,128)(2,1)S(1)} %collective-permute-done.9.refs_0_), channel_id=1, source_target_pairs={{0,1},{1,0},{2,3},{3,2},{4,5},{5,4},{6,7},{7,6},{8,9},{9,8},{10,11... | collective-permute-start | bytes 1253384 | tf_op jit(solution)/shard_map/ppermute | solution.py:21
  19.3 1.5 %collective-permute-start.27 = (bf16[272,768]{1,0:T(8,128)(2,1)S(1)}, bf16[272,768]{1,0:T(8,128)(2,1)S(1)}, u32[]{:S(2)}, u32[]{:S(2)}) collective-permute-start(bf16[272,768]{1,0:T(8,128)(2,1)S(1)} %collective-permute-done.9.refs_0_), channel_id=1, source_target_pairs={{0,2},{1,3},{2,0},{3,1},{4,6},{5,7},{6,4},{7,5},{8,10},{9,11},{10,... | collective-permute-start | bytes 1253384 | tf_op jit(solution)/shard_map/ppermute | solution.py:21
  21.8 8.5 %collective-permute-done.21.refs_1_ = bf16[272,768]{1,0:T(8,128)(2,1)S(1)} collective-permute-done((bf16[272,768]{1,0:T(8,128)(2,1)S(1)}, bf16[272,768]{1,0:T(8,128)(2,1)S(1)}, u32[]{:S(2)}, u32[]{:S(2)}) %collective-permute-start.21) | collective-permute-done | bytes 417824 | tf_op jit(solution)/shard_map/ppermute | solution.py:21
  30.3 1.6 %collective-permute-start.28 = (bf16[136,768]{1,0:T(8,128)(2,1)S(1)}, bf16[136,768]{1,0:T(8,128)(2,1)S(1)}, u32[]{:S(2)}, u32[]{:S(2)}) collective-permute-start(bf16[136,768]{1,0:T(8,128)(2,1)S(1)} %slice.52), channel_id=1, source_target_pairs={{0,2},{1,3},{2,0},{3,1},{4,6},{5,7},{6,4},{7,5},{8,10},{9,11},{10,... | collective-permute-start | bytes 626696 | tf_op jit(solution)/shard_map/ppermute | solution.py:21
  31.9 1.6 %collective-permute-start.29 = (bf16[136,768]{1,0:T(8,128)(2,1)S(1)}, bf16[136,768]{1,0:T(8,128)(2,1)S(1)}, u32[]{:S(2)}, u32[]{:S(2)}) collective-permute-start(bf16[136,768]{1,0:T(8,128)(2,1)S(1)} %slice.53), channel_id=1, source_target_pairs={{0,1},{1,0},{2,3},{3,2},{4,5},{5,4},{6,7},{7,6},{8,9},{9,8},{10,11... | collective-permute-start | bytes 626696 | tf_op jit(solution)/shard_map/ppermute | solution.py:21
  34.0 5.3 %collective-permute-done.refs_1_ = bf16[272,768]{1,0:T(8,128)(2,1)S(1)} collective-permute-done((bf16[272,768]{1,0:T(8,128)(2,1)S(1)}, bf16[272,768]{1,0:T(8,128)(2,1)S(1)}, u32[]{:S(2)}, u32[]{:S(2)}) %collective-permute-start) | collective-permute-done | bytes 417824 | tf_op jit(solution)/shard_map/ppermute | solution.py:21
  39.3 1.6 %collective-permute-start.2 = (bf16[136,768]{1,0:T(8,128)(2,1)S(1)}, bf16[136,768]{1,0:T(8,128)(2,1)S(1)}, u32[]{:S(2)}, u32[]{:S(2)}) collective-permute-start(bf16[136,768]{1,0:T(8,128)(2,1)S(1)} %slice.48), channel_id=1, source_target_pairs={{0,2},{1,3},{2,0},{3,1},{4,6},{5,7},{6,4},{7,5},{8,10},{9,11},{10,... | collective-permute-start | bytes 626696 | tf_op jit(solution)/shard_map/ppermute | solution.py:21
  40.9 1.6 %collective-permute-start.3 = (bf16[136,768]{1,0:T(8,128)(2,1)S(1)}, bf16[136,768]{1,0:T(8,128)(2,1)S(1)}, u32[]{:S(2)}, u32[]{:S(2)}) collective-permute-start(bf16[136,768]{1,0:T(8,128)(2,1)S(1)} %slice.49), channel_id=1, source_target_pairs={{0,1},{1,0},{2,3},{3,2},{4,5},{5,4},{6,7},{7,6},{8,9},{9,8},{10,11... | collective-permute-start | bytes 626696 | tf_op jit(solution)/shard_map/ppermute | solution.py:21
  42.4 3.8 %prep.1 = (bf16[3072,512]{1,0:T(8,128)(2,1)S(1)}, bf16[3072,512]{1,0:T(8,128)(2,1)S(1)}, bf16[512,3072]{1,0:T(8,128)(2,1)S(1)}) custom-call(s32[1]{0:T(128)} %bitcast.core_ref, bf16[6144,512]{1,0:T(8,128)(2,1)} %wg.1, bf16[6144,512]{1,0:T(8,128)(2,1)} %wu.1, bf16[512,6144]{1,0:T(8,128)(2,1)} %wd.1), custom_call_target="tpu_custom_call" | custom-call | tf_op jit(solution)/shard_map/prep/pallas_call | solution.py:108
  46.2 2.1 %first.7 = (f32[136,1536]{1,0:T(8,128)S(1)}, bf16[136,1536]{1,0:T(8,128)(2,1)S(1)}) custom-call(bf16[272,768]{1,0:T(8,128)(2,1)S(1)} %collective-permute-done.9.refs_0_, bf16[272,768]{1,0:T(8,128)(2,1)S(1)} %collective-permute-done.21.refs_1_, bf16[272,768]{1,0:T(8,128)(2,1)S(1)} %collective-permute-done.27.refs_2_, ...), custom_call_target="tpu_custom_call" | custom-call | tf_op jit(solution)/shard_map/first/pallas_call | solution.py:144
  48.5 7.9 %collective-permute-done.2.refs_3_ = bf16[136,768]{1,0:T(8,128)(2,1)S(1)} collective-permute-done((bf16[136,768]{1,0:T(8,128)(2,1)S(1)}, bf16[136,768]{1,0:T(8,128)(2,1)S(1)}, u32[]{:S(2)}, u32[]{:S(2)}) %collective-permute-start.2) | collective-permute-done | bytes 208928 | tf_op jit(solution)/shard_map/ppermute | solution.py:21
  56.4 2.2 %first.4 = (f32[136,1536]{1,0:T(8,128)S(1)}, bf16[136,1536]{1,0:T(8,128)(2,1)S(1)}) custom-call(bf16[272,768]{1,0:T(8,128)(2,1)S(1)} %rows.1.refs_0_, bf16[272,768]{1,0:T(8,128)(2,1)S(1)} %collective-permute-done.refs_1_, bf16[272,768]{1,0:T(8,128)(2,1)S(1)} %collective-permute-done.1.refs_2_, bf16[136,768]{1,0:T(8,128)(2,1)S(1)} %collective-permute-done.2.refs_3_, ...), custom_call_target="tpu_custom_call" | custom-call | tf_op jit(solution)/shard_map/first/pallas_call | solution.py:144
  58.8 0.8 collective-permute-start.24
  59.6 2.2 %second.7 = (bf16[136,768]{1,0:T(8,128)(2,1)S(1)}, bf16[136,768]{1,0:T(8,128)(2,1)S(1)}, bf16[136,768]{1,0:T(8,128)(2,1)S(1)}, bf16[136,768]{1,0:T(8,128)(2,1)S(1)}) custom-call(f32[136,1536]{1,0:T(8,128)S(1)} %get-tuple-element.52.mine_ref, bf16[136,1536]{1,0:T(8,128)(2,1)S(1)} %collective-permute-done.30.theirs_ref, ...), custom_call_target="tpu_custom_call" | custom-call | tf_op jit(solution)/shard_map/second/pallas_call | solution.py:179
  61.8 1.4 collective-permute-start.35
  63.1 0.7 collective-permute-start.12
  63.9 1.3 collective-permute-start.13
  65.2 2.2 %second.4 = (bf16[136,768]{1,0:T(8,128)(2,1)S(1)}, bf16[136,768]{1,0:T(8,128)(2,1)S(1)}, bf16[136,768]{1,0:T(8,128)(2,1)S(1)}, bf16[136,768]{1,0:T(8,128)(2,1)S(1)}) custom-call(f32[136,1536]{1,0:T(8,128)S(1)} %get-tuple-element.35.mine_ref, bf16[136,1536]{1,0:T(8,128)(2,1)S(1)} %collective-permute-done.4.theirs_ref, ...), custom_call_target="tpu_custom_call" | custom-call | tf_op jit(solution)/shard_map/second/pallas_call | solution.py:179
  67.4 5.1 %collective-permute-done.22.refs_1_ = bf16[272,768]{1,0:T(8,128)(2,1)S(1)} collective-permute-done((bf16[272,768]{1,0:T(8,128)(2,1)S(1)}, bf16[272,768]{1,0:T(8,128)(2,1)S(1)}, u32[]{:S(2)}, u32[]{:S(2)}) %collective-permute-start.22) | collective-permute-done | bytes 417824 | tf_op jit(solution)/shard_map/ppermute | solution.py:31
  72.5 1.5 %collective-permute-start.5 = (bf16[64,768]{1,0:T(8,128)(2,1)S(1)}, bf16[64,768]{1,0:T(8,128)(2,1)S(1)}, u32[]{:S(2)}, u32[]{:S(2)}) collective-permute-start(bf16[64,768]{1,0:T(8,128)(2,1)S(1)} %slice.38), channel_id=1, source_target_pairs={{0,2},{1,3},{2,0},{3,1},{4,6},{5,7},{6,4},{7,5},{8,10},{9,11},{10,... | collective-permute-start | bytes 294920 | tf_op jit(solution)/shard_map/ppermute | solution.py:21
  74.6 2.1 %first.6 = (f32[136,1536]{1,0:T(8,128)S(1)}, bf16[136,1536]{1,0:T(8,128)(2,1)S(1)}) custom-call(bf16[272,768]{1,0:T(8,128)(2,1)S(1)} %collective-permute-done.10.refs_0_, bf16[272,768]{1,0:T(8,128)(2,1)S(1)} %collective-permute-done.22.refs_1_, bf16[272,768]{1,0:T(8,128)(2,1)S(1)} %collective-permute-done.23.refs_2_, ...), custom_call_target="tpu_custom_call" | custom-call | tf_op jit(solution)/shard_map/first/pallas_call | solution.py:144
  76.9 7.9 %collective-permute-done.12.refs_1_ = bf16[272,768]{1,0:T(8,128)(2,1)S(1)} collective-permute-done((bf16[272,768]{1,0:T(8,128)(2,1)S(1)}, bf16[272,768]{1,0:T(8,128)(2,1)S(1)}, u32[]{:S(2)}, u32[]{:S(2)}) %collective-permute-start.12) | collective-permute-done | bytes 417824 | tf_op jit(solution)/shard_map/ppermute | solution.py:21
  84.8 1.5 %collective-permute-start.36 = (bf16[136,768]{1,0:T(8,128)(2,1)S(1)}, bf16[136,768]{1,0:T(8,128)(2,1)S(1)}, u32[]{:S(2)}, u32[]{:S(2)}) collective-permute-start(bf16[136,768]{1,0:T(8,128)(2,1)S(1)} %add_convert_fusion.3), channel_id=1, source_target_pairs={{0,2},{1,3},{2,0},{3,1},{4,6},{5,7},{6,4},{7,5},{8,10},{9,11},{10,... | collective-permute-start | bytes 626696 | tf_op jit(solution)/shard_map/ppermute | solution.py:21
  86.9 0.8 collective-permute-start.15
  87.8 7.5 %collective-permute-done.14.refs_3_ = bf16[136,768]{1,0:T(8,128)(2,1)S(1)} collective-permute-done((bf16[136,768]{1,0:T(8,128)(2,1)S(1)}, bf16[136,768]{1,0:T(8,128)(2,1)S(1)}, u32[]{:S(2)}, u32[]{:S(2)}) %collective-permute-start.14) | collective-permute-done | bytes 208928 | tf_op jit(solution)/shard_map/ppermute | solution.py:21
  95.2 0.7 collective-permute-start.6
  96.5 2.1 %first.5 = (f32[136,1536]{1,0:T(8,128)S(1)}, bf16[136,1536]{1,0:T(8,128)(2,1)S(1)}) custom-call(bf16[272,768]{1,0:T(8,128)(2,1)S(1)} %collective-permute-done.11.refs_0_, bf16[272,768]{1,0:T(8,128)(2,1)S(1)} %collective-permute-done.12.refs_1_, bf16[272,768]{1,0:T(8,128)(2,1)S(1)} %collective-permute-done.13.refs_2_, ...), custom_call_target="tpu_custom_call" | custom-call | tf_op jit(solution)/shard_map/first/pallas_call | solution.py:144
  98.8 2.2 %second.6 = (bf16[136,768]{1,0:T(8,128)(2,1)S(1)}, bf16[136,768]{1,0:T(8,128)(2,1)S(1)}, bf16[136,768]{1,0:T(8,128)(2,1)S(1)}, bf16[136,768]{1,0:T(8,128)(2,1)S(1)}) custom-call(f32[136,1536]{1,0:T(8,128)S(1)} %get-tuple-element.47.mine_ref, bf16[136,1536]{1,0:T(8,128)(2,1)S(1)} %collective-permute-done.25.theirs_ref, ...), custom_call_target="tpu_custom_call" | custom-call | tf_op jit(solution)/shard_map/second/pallas_call | solution.py:179
  101.0 1.6 %collective-permute-start.26 = (bf16[64,768]{1,0:T(8,128)(2,1)S(1)}, bf16[64,768]{1,0:T(8,128)(2,1)S(1)}, u32[]{:S(2)}, u32[]{:S(2)}) collective-permute-start(bf16[64,768]{1,0:T(8,128)(2,1)S(1)} %slice.44), channel_id=1, source_target_pairs={{0,2},{1,3},{2,0},{3,1},{4,6},{5,7},{6,4},{7,5},{8,10},{9,11},{10,... | collective-permute-start | bytes 294920 | tf_op jit(solution)/shard_map/ppermute | solution.py:21
  102.6 0.9 collective-permute-done.31
  104.3 1.9 %collective-permute-done.26 = bf16[64,768]{1,0:T(8,128)(2,1)S(1)} collective-permute-done((bf16[64,768]{1,0:T(8,128)(2,1)S(1)}, bf16[64,768]{1,0:T(8,128)(2,1)S(1)}, u32[]{:S(2)}, u32[]{:S(2)}) %collective-permute-start.26) | collective-permute-done | bytes 98336 | tf_op jit(solution)/shard_map/ppermute | solution.py:21
  106.2 1.5 %collective-permute-start.33 = (bf16[72,768]{1,0:T(8,128)(2,1)S(1)}, bf16[72,768]{1,0:T(8,128)(2,1)S(1)}, u32[]{:S(2)}, u32[]{:S(2)}) collective-permute-start(bf16[72,768]{1,0:T(8,128)(2,1)S(1)} %slice.47), channel_id=1, source_target_pairs={{0,1},{1,0},{2,3},{3,2},{4,5},{5,4},{6,7},{7,6},{8,9},{9,8},{10,11... | collective-permute-start | bytes 331784 | tf_op jit(solution)/shard_map/ppermute | solution.py:21
  108.4 2.2 %second.5 = (bf16[136,768]{1,0:T(8,128)(2,1)S(1)}, bf16[136,768]{1,0:T(8,128)(2,1)S(1)}, bf16[136,768]{1,0:T(8,128)(2,1)S(1)}, bf16[136,768]{1,0:T(8,128)(2,1)S(1)}) custom-call(f32[136,1536]{1,0:T(8,128)S(1)} %get-tuple-element.41.mine_ref, bf16[136,1536]{1,0:T(8,128)(2,1)S(1)} %collective-permute-done.16.theirs_ref, ...), custom_call_target="tpu_custom_call" | custom-call | tf_op jit(solution)/shard_map/second/pallas_call | solution.py:179
  110.7 1.5 %collective-permute-done.33 = bf16[72,768]{1,0:T(8,128)(2,1)S(1)} collective-permute-done((bf16[72,768]{1,0:T(8,128)(2,1)S(1)}, bf16[72,768]{1,0:T(8,128)(2,1)S(1)}, u32[]{:S(2)}, u32[]{:S(2)}) %collective-permute-start.33) | collective-permute-done | bytes 110624 | tf_op jit(solution)/shard_map/ppermute | solution.py:21
  112.1 1.5 %collective-permute-start.17 = (bf16[64,768]{1,0:T(8,128)(2,1)S(1)}, bf16[64,768]{1,0:T(8,128)(2,1)S(1)}, u32[]{:S(2)}, u32[]{:S(2)}) collective-permute-start(bf16[64,768]{1,0:T(8,128)(2,1)S(1)} %slice.42), channel_id=1, source_target_pairs={{0,2},{1,3},{2,0},{3,1},{4,6},{5,7},{6,4},{7,5},{8,10},{9,11},{10,... | collective-permute-start | bytes 294920 | tf_op jit(solution)/shard_map/ppermute | solution.py:21
  113.7 3.7 %collective-permute-done.17 = bf16[64,768]{1,0:T(8,128)(2,1)S(1)} collective-permute-done((bf16[64,768]{1,0:T(8,128)(2,1)S(1)}, bf16[64,768]{1,0:T(8,128)(2,1)S(1)}, u32[]{:S(2)}, u32[]{:S(2)}) %collective-permute-start.17) | collective-permute-done | bytes 98336 | tf_op jit(solution)/shard_map/ppermute | solution.py:21
  117.4 1.5 %collective-permute-start.34 = (bf16[136,768]{1,0:T(8,128)(2,1)S(1)}, bf16[136,768]{1,0:T(8,128)(2,1)S(1)}, u32[]{:S(2)}, u32[]{:S(2)}) collective-permute-start(bf16[136,768]{1,0:T(8,128)(2,1)S(1)} %add_convert_fusion.4), channel_id=1, source_target_pairs={{0,2},{1,3},{2,0},{3,1},{4,6},{5,7},{6,4},{7,5},{8,10},{9,11},{10,... | collective-permute-start | bytes 626696 | tf_op jit(solution)/shard_map/ppermute | solution.py:21
  118.9 1.6 %collective-permute-start.19 = (bf16[72,768]{1,0:T(8,128)(2,1)S(1)}, bf16[72,768]{1,0:T(8,128)(2,1)S(1)}, u32[]{:S(2)}, u32[]{:S(2)}) collective-permute-start(bf16[72,768]{1,0:T(8,128)(2,1)S(1)} %slice.43), channel_id=1, source_target_pairs={{0,1},{1,0},{2,3},{3,2},{4,5},{5,4},{6,7},{7,6},{8,9},{9,8},{10,11... | collective-permute-start | bytes 331784 | tf_op jit(solution)/shard_map/ppermute | solution.py:21
  121.0 2.3 %collective-permute-done.34 = bf16[136,768]{1,0:T(8,128)(2,1)S(1)} collective-permute-done((bf16[136,768]{1,0:T(8,128)(2,1)S(1)}, bf16[136,768]{1,0:T(8,128)(2,1)S(1)}, u32[]{:S(2)}, u32[]{:S(2)}) %collective-permute-start.34) | collective-permute-done | bytes 208928 | tf_op jit(solution)/shard_map/ppermute | solution.py:21
  123.4 1.5 %collective-permute-start.38 = (bf16[136,768]{1,0:T(8,128)(2,1)S(1)}, bf16[136,768]{1,0:T(8,128)(2,1)S(1)}, u32[]{:S(2)}, u32[]{:S(2)}) collective-permute-start(bf16[136,768]{1,0:T(8,128)(2,1)S(1)} %add_convert_fusion.1), channel_id=1, source_target_pairs={{0,4},{1,5},{2,6},{3,7},{4,8},{5,9},{6,10},{7,11},{8,12},{9,13},{1... | collective-permute-start | bytes 626696 | tf_op jit(solution)/shard_map/ppermute | solution.py:31
  125.0 1.6 %collective-permute-start.20 = (bf16[136,768]{1,0:T(8,128)(2,1)S(1)}, bf16[136,768]{1,0:T(8,128)(2,1)S(1)}, u32[]{:S(2)}, u32[]{:S(2)}) collective-permute-start(bf16[136,768]{1,0:T(8,128)(2,1)S(1)} %add_convert_fusion.6), channel_id=1, source_target_pairs={{0,2},{1,3},{2,0},{3,1},{4,6},{5,7},{6,4},{7,5},{8,10},{9,11},{10,... | collective-permute-start | bytes 626696 | tf_op jit(solution)/shard_map/ppermute | solution.py:21
  127.2 6.1 %collective-permute-done.38 = bf16[136,768]{1,0:T(8,128)(2,1)S(1)} collective-permute-done((bf16[136,768]{1,0:T(8,128)(2,1)S(1)}, bf16[136,768]{1,0:T(8,128)(2,1)S(1)}, u32[]{:S(2)}, u32[]{:S(2)}) %collective-permute-start.38) | collective-permute-done | bytes 208928 | tf_op jit(solution)/shard_map/ppermute | solution.py:31
  133.4 1.3 collective-permute-start.39
  134.7 6.4 %collective-permute-done.39.sz_ref = bf16[136,768]{1,0:T(8,128)(2,1)S(1)} collective-permute-done((bf16[136,768]{1,0:T(8,128)(2,1)S(1)}, bf16[136,768]{1,0:T(8,128)(2,1)S(1)}, u32[]{:S(2)}, u32[]{:S(2)}) %collective-permute-start.39) | collective-permute-done | bytes 208928 | tf_op jit(solution)/shard_map/ppermute | solution.py:31
  141.1 2.6 %last.1 = bf16[128,3072]{1,0:T(8,128)(2,1)} custom-call(s32[1]{0:T(128)} %bitcast.core_ref, s32[1]{0:T(128)S(6)} %copy.9.fe_ref, s32[2,128]{1,0:T(2,128)S(1)} %bitcast.4, f32[2,128]{1,0:T(2,128)S(1)} %bitcast.5, bf16[128,6144]{1,0:T(8,128)(2,1)} %grad_hbm.1, bf16[136,768]{1,0:T(8,128)(2,1)S(1)} %get-tuple-element.37.p0_ref, ...), custom_call_target="tpu_custom_call" | custom-call | tf_op jit(solution)/shard_map/last/pallas_call | solution.py:214
  (71 shorter events, 7.4 us)
Async XLA Ops:
  0.7 0.7 copy-start
  3.0 14.8 %collective-permute-start.9 = (bf16[272,768]{1,0:T(8,128)(2,1)S(1)}, bf16[272,768]{1,0:T(8,128)(2,1)S(1)}, u32[]{:S(2)}, u32[]{:S(2)}) collective-permute-start(bf16[272,768]{1,0:T(8,128)(2,1)S(1)} %rows.1.refs_0_), channel_id=1, source_target_pairs={{0,4},{1,5},{2,6},{3,7},{4,8},{5,9},{6,10},{7,11},{8,12},{9,13},{1... | collective-permute-start | bytes 1253384 | tf_op jit(solution)/shard_map/ppermute | solution.py:31
  17.8 12.5 %collective-permute-start.21 = (bf16[272,768]{1,0:T(8,128)(2,1)S(1)}, bf16[272,768]{1,0:T(8,128)(2,1)S(1)}, u32[]{:S(2)}, u32[]{:S(2)}) collective-permute-start(bf16[272,768]{1,0:T(8,128)(2,1)S(1)} %collective-permute-done.9.refs_0_), channel_id=1, source_target_pairs={{0,1},{1,0},{2,3},{3,2},{4,5},{5,4},{6,7},{7,6},{8,9},{9,8},{10,11... | collective-permute-start | bytes 1253384 | tf_op jit(solution)/shard_map/ppermute | solution.py:21
  19.3 12.6 %collective-permute-start.27 = (bf16[272,768]{1,0:T(8,128)(2,1)S(1)}, bf16[272,768]{1,0:T(8,128)(2,1)S(1)}, u32[]{:S(2)}, u32[]{:S(2)}) collective-permute-start(bf16[272,768]{1,0:T(8,128)(2,1)S(1)} %collective-permute-done.9.refs_0_), channel_id=1, source_target_pairs={{0,2},{1,3},{2,0},{3,1},{4,6},{5,7},{6,4},{7,5},{8,10},{9,11},{10,... | collective-permute-start | bytes 1253384 | tf_op jit(solution)/shard_map/ppermute | solution.py:21
  20.8 12.7 %collective-permute-start.10 = (bf16[272,768]{1,0:T(8,128)(2,1)S(1)}, bf16[272,768]{1,0:T(8,128)(2,1)S(1)}, u32[]{:S(2)}, u32[]{:S(2)}) collective-permute-start(bf16[272,768]{1,0:T(8,128)(2,1)S(1)} %collective-permute-done.9.refs_0_), channel_id=1, source_target_pairs={{0,4},{1,5},{2,6},{3,7},{4,8},{5,9},{6,10},{7,11},{8,12},{9,13},{1... | collective-permute-start | bytes 1253384 | tf_op jit(solution)/shard_map/ppermute | solution.py:31
  20.8 18.4 %collective-permute-start = (bf16[272,768]{1,0:T(8,128)(2,1)S(1)}, bf16[272,768]{1,0:T(8,128)(2,1)S(1)}, u32[]{:S(2)}, u32[]{:S(2)}) collective-permute-start(bf16[272,768]{1,0:T(8,128)(2,1)S(1)} %rows.1.refs_0_), channel_id=1, source_target_pairs={{0,1},{1,0},{2,3},{3,2},{4,5},{5,4},{6,7},{7,6},{8,9},{9,8},{10,11... | collective-permute-start | bytes 1253384 | tf_op jit(solution)/shard_map/ppermute | solution.py:21
  21.3 19.5 %collective-permute-start.1 = (bf16[272,768]{1,0:T(8,128)(2,1)S(1)}, bf16[272,768]{1,0:T(8,128)(2,1)S(1)}, u32[]{:S(2)}, u32[]{:S(2)}) collective-permute-start(bf16[272,768]{1,0:T(8,128)(2,1)S(1)} %rows.1.refs_0_), channel_id=1, source_target_pairs={{0,2},{1,3},{2,0},{3,1},{4,6},{5,7},{6,4},{7,5},{8,10},{9,11},{10,... | collective-permute-start | bytes 1253384 | tf_op jit(solution)/shard_map/ppermute | solution.py:21
  30.3 15.9 %collective-permute-start.28 = (bf16[136,768]{1,0:T(8,128)(2,1)S(1)}, bf16[136,768]{1,0:T(8,128)(2,1)S(1)}, u32[]{:S(2)}, u32[]{:S(2)}) collective-permute-start(bf16[136,768]{1,0:T(8,128)(2,1)S(1)} %slice.52), channel_id=1, source_target_pairs={{0,2},{1,3},{2,0},{3,1},{4,6},{5,7},{6,4},{7,5},{8,10},{9,11},{10,... | collective-permute-start | bytes 626696 | tf_op jit(solution)/shard_map/ppermute | solution.py:21
  31.9 14.3 %collective-permute-start.29 = (bf16[136,768]{1,0:T(8,128)(2,1)S(1)}, bf16[136,768]{1,0:T(8,128)(2,1)S(1)}, u32[]{:S(2)}, u32[]{:S(2)}) collective-permute-start(bf16[136,768]{1,0:T(8,128)(2,1)S(1)} %slice.53), channel_id=1, source_target_pairs={{0,1},{1,0},{2,3},{3,2},{4,5},{5,4},{6,7},{7,6},{8,9},{9,8},{10,11... | collective-permute-start | bytes 626696 | tf_op jit(solution)/shard_map/ppermute | solution.py:21
  33.5 25.3 %collective-permute-start.23 = (bf16[272,768]{1,0:T(8,128)(2,1)S(1)}, bf16[272,768]{1,0:T(8,128)(2,1)S(1)}, u32[]{:S(2)}, u32[]{:S(2)}) collective-permute-start(bf16[272,768]{1,0:T(8,128)(2,1)S(1)} %collective-permute-done.10.refs_0_), channel_id=1, source_target_pairs={{0,2},{1,3},{2,0},{3,1},{4,6},{5,7},{6,4},{7,5},{8,10},{9,11},{10,... | collective-permute-start | bytes 1253384 | tf_op jit(solution)/shard_map/ppermute | solution.py:21
  39.3 17.2 %collective-permute-start.2 = (bf16[136,768]{1,0:T(8,128)(2,1)S(1)}, bf16[136,768]{1,0:T(8,128)(2,1)S(1)}, u32[]{:S(2)}, u32[]{:S(2)}) collective-permute-start(bf16[136,768]{1,0:T(8,128)(2,1)S(1)} %slice.48), channel_id=1, source_target_pairs={{0,2},{1,3},{2,0},{3,1},{4,6},{5,7},{6,4},{7,5},{8,10},{9,11},{10,... | collective-permute-start | bytes 626696 | tf_op jit(solution)/shard_map/ppermute | solution.py:21
  40.9 15.6 %collective-permute-start.3 = (bf16[136,768]{1,0:T(8,128)(2,1)S(1)}, bf16[136,768]{1,0:T(8,128)(2,1)S(1)}, u32[]{:S(2)}, u32[]{:S(2)}) collective-permute-start(bf16[136,768]{1,0:T(8,128)(2,1)S(1)} %slice.49), channel_id=1, source_target_pairs={{0,1},{1,0},{2,3},{3,2},{4,5},{5,4},{6,7},{7,6},{8,9},{9,8},{10,11... | collective-permute-start | bytes 626696 | tf_op jit(solution)/shard_map/ppermute | solution.py:21
  48.4 11.2 %collective-permute-start.30 = (bf16[136,1536]{1,0:T(8,128)(2,1)S(1)}, bf16[136,1536]{1,0:T(8,128)(2,1)S(1)}, u32[]{:S(2)}, u32[]{:S(2)}) collective-permute-start(bf16[136,1536]{1,0:T(8,128)(2,1)S(1)} %get-tuple-element.53), channel_id=1, source_target_pairs={{0,16},{16,0},{1,17},{17,1},{2,18},{18,2},{3,19},{19,3},{4,20},{20... | collective-permute-start | bytes 1253384 | tf_op jit(solution)/shard_map/ppermute | solution.py:226
  48.5 14.7 %collective-permute-start.11 = (bf16[272,768]{1,0:T(8,128)(2,1)S(1)}, bf16[272,768]{1,0:T(8,128)(2,1)S(1)}, u32[]{:S(2)}, u32[]{:S(2)}) collective-permute-start(bf16[272,768]{1,0:T(8,128)(2,1)S(1)} %collective-permute-done.10.refs_0_), channel_id=1, source_target_pairs={{0,4},{1,5},{2,6},{3,7},{4,8},{5,9},{6,10},{7,11},{8,12},{9,13},{1... | collective-permute-start | bytes 1253384 | tf_op jit(solution)/shard_map/ppermute | solution.py:31
  58.6 5.3 %collective-permute-start.4 = (bf16[136,1536]{1,0:T(8,128)(2,1)S(1)}, bf16[136,1536]{1,0:T(8,128)(2,1)S(1)}, u32[]{:S(2)}, u32[]{:S(2)}) collective-permute-start(bf16[136,1536]{1,0:T(8,128)(2,1)S(1)} %get-tuple-element.36), channel_id=1, source_target_pairs={{0,16},{16,0},{1,17},{17,1},{2,18},{18,2},{3,19},{19,3},{4,20},{20... | collective-permute-start | bytes 1253384 | tf_op jit(solution)/shard_map/ppermute | solution.py:226
  58.7 13.8 %collective-permute-start.22 = (bf16[272,768]{1,0:T(8,128)(2,1)S(1)}, bf16[272,768]{1,0:T(8,128)(2,1)S(1)}, u32[]{:S(2)}, u32[]{:S(2)}) collective-permute-start(bf16[272,768]{1,0:T(8,128)(2,1)S(1)} %collective-permute-done.21.refs_1_), channel_id=1, source_target_pairs={{0,4},{1,5},{2,6},{3,7},{4,8},{5,9},{6,10},{7,11},{8,12},{9,13},{1... | collective-permute-start | bytes 1253384 | tf_op jit(solution)/shard_map/ppermute | solution.py:31
  58.8 15.3 %collective-permute-start.24 = (bf16[272,768]{1,0:T(8,128)(2,1)S(1)}, bf16[272,768]{1,0:T(8,128)(2,1)S(1)}, u32[]{:S(2)}, u32[]{:S(2)}) collective-permute-start(bf16[272,768]{1,0:T(8,128)(2,1)S(1)} %collective-permute-done.23.refs_2_), channel_id=1, source_target_pairs={{0,1},{1,0},{2,3},{3,2},{4,5},{5,4},{6,7},{7,6},{8,9},{9,8},{10,11... | collective-permute-start | bytes 1253384 | tf_op jit(solution)/shard_map/ppermute | solution.py:21
  61.8 15.0 %collective-permute-start.35 = (bf16[136,768]{1,0:T(8,128)(2,1)S(1)}, bf16[136,768]{1,0:T(8,128)(2,1)S(1)}, u32[]{:S(2)}, u32[]{:S(2)}) collective-permute-start(bf16[136,768]{1,0:T(8,128)(2,1)S(1)} %get-tuple-element.58), channel_id=1, source_target_pairs={{0,1},{1,0},{2,3},{3,2},{4,5},{5,4},{6,7},{7,6},{8,9},{9,8},{10,11... | collective-permute-start | bytes 626696 | tf_op jit(solution)/shard_map/ppermute | solution.py:21
  63.1 21.6 %collective-permute-start.12 = (bf16[272,768]{1,0:T(8,128)(2,1)S(1)}, bf16[272,768]{1,0:T(8,128)(2,1)S(1)}, u32[]{:S(2)}, u32[]{:S(2)}) collective-permute-start(bf16[272,768]{1,0:T(8,128)(2,1)S(1)} %collective-permute-done.11.refs_0_), channel_id=1, source_target_pairs={{0,1},{1,0},{2,3},{3,2},{4,5},{5,4},{6,7},{7,6},{8,9},{9,8},{10,11... | collective-permute-start | bytes 1253384 | tf_op jit(solution)/shard_map/ppermute | solution.py:21
  63.9 22.4 %collective-permute-start.13 = (bf16[272,768]{1,0:T(8,128)(2,1)S(1)}, bf16[272,768]{1,0:T(8,128)(2,1)S(1)}, u32[]{:S(2)}, u32[]{:S(2)}) collective-permute-start(bf16[272,768]{1,0:T(8,128)(2,1)S(1)} %collective-permute-done.11.refs_0_), channel_id=1, source_target_pairs={{0,2},{1,3},{2,0},{3,1},{4,6},{5,7},{6,4},{7,5},{8,10},{9,11},{10,... | collective-permute-start | bytes 1253384 | tf_op jit(solution)/shard_map/ppermute | solution.py:21
  72.5 14.4 %collective-permute-start.5 = (bf16[64,768]{1,0:T(8,128)(2,1)S(1)}, bf16[64,768]{1,0:T(8,128)(2,1)S(1)}, u32[]{:S(2)}, u32[]{:S(2)}) collective-permute-start(bf16[64,768]{1,0:T(8,128)(2,1)S(1)} %slice.38), channel_id=1, source_target_pairs={{0,2},{1,3},{2,0},{3,1},{4,6},{5,7},{6,4},{7,5},{8,10},{9,11},{10,... | collective-permute-start | bytes 294920 | tf_op jit(solution)/shard_map/ppermute | solution.py:21
  74.1 52.5 %collective-permute-start.7 = (bf16[72,768]{1,0:T(8,128)(2,1)S(1)}, bf16[72,768]{1,0:T(8,128)(2,1)S(1)}, u32[]{:S(2)}, u32[]{:S(2)}) collective-permute-start(bf16[72,768]{1,0:T(8,128)(2,1)S(1)} %slice.39), channel_id=1, source_target_pairs={{0,1},{1,0},{2,3},{3,2},{4,5},{5,4},{6,7},{7,6},{8,9},{9,8},{10,11... | collective-permute-start | bytes 331784 | tf_op jit(solution)/shard_map/ppermute | solution.py:21
  76.7 21.9 %collective-permute-start.25 = (bf16[136,1536]{1,0:T(8,128)(2,1)S(1)}, bf16[136,1536]{1,0:T(8,128)(2,1)S(1)}, u32[]{:S(2)}, u32[]{:S(2)}) collective-permute-start(bf16[136,1536]{1,0:T(8,128)(2,1)S(1)} %get-tuple-element.48), channel_id=1, source_target_pairs={{0,16},{16,0},{1,17},{17,1},{2,18},{18,2},{3,19},{19,3},{4,20},{20... | collective-permute-start | bytes 1253384 | tf_op jit(solution)/shard_map/ppermute | solution.py:226
  84.8 16.2 %collective-permute-start.36 = (bf16[136,768]{1,0:T(8,128)(2,1)S(1)}, bf16[136,768]{1,0:T(8,128)(2,1)S(1)}, u32[]{:S(2)}, u32[]{:S(2)}) collective-permute-start(bf16[136,768]{1,0:T(8,128)(2,1)S(1)} %add_convert_fusion.3), channel_id=1, source_target_pairs={{0,2},{1,3},{2,0},{3,1},{4,6},{5,7},{6,4},{7,5},{8,10},{9,11},{10,... | collective-permute-start | bytes 626696 | tf_op jit(solution)/shard_map/ppermute | solution.py:21
  86.3 8.9 %collective-permute-start.14 = (bf16[136,768]{1,0:T(8,128)(2,1)S(1)}, bf16[136,768]{1,0:T(8,128)(2,1)S(1)}, u32[]{:S(2)}, u32[]{:S(2)}) collective-permute-start(bf16[136,768]{1,0:T(8,128)(2,1)S(1)} %slice.50), channel_id=1, source_target_pairs={{0,2},{1,3},{2,0},{3,1},{4,6},{5,7},{6,4},{7,5},{8,10},{9,11},{10,... | collective-permute-start | bytes 626696 | tf_op jit(solution)/shard_map/ppermute | solution.py:21
  86.9 9.0 %collective-permute-start.15 = (bf16[136,768]{1,0:T(8,128)(2,1)S(1)}, bf16[136,768]{1,0:T(8,128)(2,1)S(1)}, u32[]{:S(2)}, u32[]{:S(2)}) collective-permute-start(bf16[136,768]{1,0:T(8,128)(2,1)S(1)} %slice.51), channel_id=1, source_target_pairs={{0,1},{1,0},{2,3},{3,2},{4,5},{5,4},{6,7},{7,6},{8,9},{9,8},{10,11... | collective-permute-start | bytes 626696 | tf_op jit(solution)/shard_map/ppermute | solution.py:21
  95.2 39.5 %collective-permute-start.6 = (bf16[136,768]{1,0:T(8,128)(2,1)S(1)}, bf16[136,768]{1,0:T(8,128)(2,1)S(1)}, u32[]{:S(2)}, u32[]{:S(2)}) collective-permute-start(bf16[136,768]{1,0:T(8,128)(2,1)S(1)} %add_convert_fusion.9), channel_id=1, source_target_pairs={{0,1},{1,0},{2,3},{3,2},{4,5},{5,4},{6,7},{7,6},{8,9},{9,8},{10,11... | collective-permute-start | bytes 626696 | tf_op jit(solution)/shard_map/ppermute | solution.py:21
  96.0 7.6 %collective-permute-start.31 = (bf16[136,768]{1,0:T(8,128)(2,1)S(1)}, bf16[136,768]{1,0:T(8,128)(2,1)S(1)}, u32[]{:S(2)}, u32[]{:S(2)}) collective-permute-start(bf16[136,768]{1,0:T(8,128)(2,1)S(1)} %get-tuple-element.54), channel_id=1, source_target_pairs={{0,4},{1,5},{2,6},{3,7},{4,8},{5,9},{6,10},{7,11},{8,12},{9,13},{1... | collective-permute-start | bytes 626696 | tf_op jit(solution)/shard_map/ppermute | solution.py:31
  98.7 9.1 %collective-permute-start.16 = (bf16[136,1536]{1,0:T(8,128)(2,1)S(1)}, bf16[136,1536]{1,0:T(8,128)(2,1)S(1)}, u32[]{:S(2)}, u32[]{:S(2)}) collective-permute-start(bf16[136,1536]{1,0:T(8,128)(2,1)S(1)} %get-tuple-element.42), channel_id=1, source_target_pairs={{0,16},{16,0},{1,17},{17,1},{2,18},{18,2},{3,19},{19,3},{4,20},{20... | collective-permute-start | bytes 1253384 | tf_op jit(solution)/shard_map/ppermute | solution.py:226
  101.0 5.3 %collective-permute-start.26 = (bf16[64,768]{1,0:T(8,128)(2,1)S(1)}, bf16[64,768]{1,0:T(8,128)(2,1)S(1)}, u32[]{:S(2)}, u32[]{:S(2)}) collective-permute-start(bf16[64,768]{1,0:T(8,128)(2,1)S(1)} %slice.44), channel_id=1, source_target_pairs={{0,2},{1,3},{2,0},{3,1},{4,6},{5,7},{6,4},{7,5},{8,10},{9,11},{10,... | collective-permute-start | bytes 294920 | tf_op jit(solution)/shard_map/ppermute | solution.py:21
  103.6 15.3 %collective-permute-start.37 = (bf16[136,768]{1,0:T(8,128)(2,1)S(1)}, bf16[136,768]{1,0:T(8,128)(2,1)S(1)}, u32[]{:S(2)}, u32[]{:S(2)}) collective-permute-start(bf16[136,768]{1,0:T(8,128)(2,1)S(1)} %add_convert_fusion.2), channel_id=1, source_target_pairs={{0,4},{1,5},{2,6},{3,7},{4,8},{5,9},{6,10},{7,11},{8,12},{9,13},{1... | collective-permute-start | bytes 626696 | tf_op jit(solution)/shard_map/ppermute | solution.py:31
  106.2 5.9 %collective-permute-start.33 = (bf16[72,768]{1,0:T(8,128)(2,1)S(1)}, bf16[72,768]{1,0:T(8,128)(2,1)S(1)}, u32[]{:S(2)}, u32[]{:S(2)}) collective-permute-start(bf16[72,768]{1,0:T(8,128)(2,1)S(1)} %slice.47), channel_id=1, source_target_pairs={{0,1},{1,0},{2,3},{3,2},{4,5},{5,4},{6,7},{7,6},{8,9},{9,8},{10,11... | collective-permute-start | bytes 331784 | tf_op jit(solution)/shard_map/ppermute | solution.py:21
  107.8 12.7 %collective-permute-start.32 = (bf16[136,768]{1,0:T(8,128)(2,1)S(1)}, bf16[136,768]{1,0:T(8,128)(2,1)S(1)}, u32[]{:S(2)}, u32[]{:S(2)}) collective-permute-start(bf16[136,768]{1,0:T(8,128)(2,1)S(1)} %add_convert_fusion.5), channel_id=1, source_target_pairs={{0,1},{1,0},{2,3},{3,2},{4,5},{5,4},{6,7},{7,6},{8,9},{9,8},{10,11... | collective-permute-start | bytes 626696 | tf_op jit(solution)/shard_map/ppermute | solution.py:21
  110.6 30.5 %copy-start.1 = (s32[128,2]{0,1:T(2,128)S(1)}, s32[128,2]{0,1:T(2,128)}, u32[]{:S(2)}) copy-start(s32[128,2]{0,1:T(2,128)} %param.10) | copy-start | bytes 3076
  110.6 30.5 %copy-start.2 = (f32[128,2]{0,1:T(2,128)S(1)}, f32[128,2]{0,1:T(2,128)}, u32[]{:S(2)}) copy-start(f32[128,2]{0,1:T(2,128)} %param.11) | copy-start | bytes 3076
  112.1 5.2 %collective-permute-start.17 = (bf16[64,768]{1,0:T(8,128)(2,1)S(1)}, bf16[64,768]{1,0:T(8,128)(2,1)S(1)}, u32[]{:S(2)}, u32[]{:S(2)}) collective-permute-start(bf16[64,768]{1,0:T(8,128)(2,1)S(1)} %slice.42), channel_id=1, source_target_pairs={{0,2},{1,3},{2,0},{3,1},{4,6},{5,7},{6,4},{7,5},{8,10},{9,11},{10,... | collective-permute-start | bytes 294920 | tf_op jit(solution)/shard_map/ppermute | solution.py:21
  117.4 5.9 %collective-permute-start.34 = (bf16[136,768]{1,0:T(8,128)(2,1)S(1)}, bf16[136,768]{1,0:T(8,128)(2,1)S(1)}, u32[]{:S(2)}, u32[]{:S(2)}) collective-permute-start(bf16[136,768]{1,0:T(8,128)(2,1)S(1)} %add_convert_fusion.4), channel_id=1, source_target_pairs={{0,2},{1,3},{2,0},{3,1},{4,6},{5,7},{6,4},{7,5},{8,10},{9,11},{10,... | collective-permute-start | bytes 626696 | tf_op jit(solution)/shard_map/ppermute | solution.py:21
  118.9 6.1 %collective-permute-start.19 = (bf16[72,768]{1,0:T(8,128)(2,1)S(1)}, bf16[72,768]{1,0:T(8,128)(2,1)S(1)}, u32[]{:S(2)}, u32[]{:S(2)}) collective-permute-start(bf16[72,768]{1,0:T(8,128)(2,1)S(1)} %slice.43), channel_id=1, source_target_pairs={{0,1},{1,0},{2,3},{3,2},{4,5},{5,4},{6,7},{7,6},{8,9},{9,8},{10,11... | collective-permute-start | bytes 331784 | tf_op jit(solution)/shard_map/ppermute | solution.py:21
  120.5 6.7 %collective-permute-start.18 = (bf16[136,768]{1,0:T(8,128)(2,1)S(1)}, bf16[136,768]{1,0:T(8,128)(2,1)S(1)}, u32[]{:S(2)}, u32[]{:S(2)}) collective-permute-start(bf16[136,768]{1,0:T(8,128)(2,1)S(1)} %add_convert_fusion.7), channel_id=1, source_target_pairs={{0,1},{1,0},{2,3},{3,2},{4,5},{5,4},{6,7},{7,6},{8,9},{9,8},{10,11... | collective-permute-start | bytes 626696 | tf_op jit(solution)/shard_map/ppermute | solution.py:21
  123.4 9.9 %collective-permute-start.38 = (bf16[136,768]{1,0:T(8,128)(2,1)S(1)}, bf16[136,768]{1,0:T(8,128)(2,1)S(1)}, u32[]{:S(2)}, u32[]{:S(2)}) collective-permute-start(bf16[136,768]{1,0:T(8,128)(2,1)S(1)} %add_convert_fusion.1), channel_id=1, source_target_pairs={{0,4},{1,5},{2,6},{3,7},{4,8},{5,9},{6,10},{7,11},{8,12},{9,13},{1... | collective-permute-start | bytes 626696 | tf_op jit(solution)/shard_map/ppermute | solution.py:31
  125.0 8.3 %collective-permute-start.20 = (bf16[136,768]{1,0:T(8,128)(2,1)S(1)}, bf16[136,768]{1,0:T(8,128)(2,1)S(1)}, u32[]{:S(2)}, u32[]{:S(2)}) collective-permute-start(bf16[136,768]{1,0:T(8,128)(2,1)S(1)} %add_convert_fusion.6), channel_id=1, source_target_pairs={{0,2},{1,3},{2,0},{3,1},{4,6},{5,7},{6,4},{7,5},{8,10},{9,11},{10,... | collective-permute-start | bytes 626696 | tf_op jit(solution)/shard_map/ppermute | solution.py:21
  126.6 8.1 %collective-permute-start.8 = (bf16[136,768]{1,0:T(8,128)(2,1)S(1)}, bf16[136,768]{1,0:T(8,128)(2,1)S(1)}, u32[]{:S(2)}, u32[]{:S(2)}) collective-permute-start(bf16[136,768]{1,0:T(8,128)(2,1)S(1)} %add_convert_fusion.8), channel_id=1, source_target_pairs={{0,2},{1,3},{2,0},{3,1},{4,6},{5,7},{6,4},{7,5},{8,10},{9,11},{10,... | collective-permute-start | bytes 626696 | tf_op jit(solution)/shard_map/ppermute | solution.py:21
  133.4 7.7 %collective-permute-start.39 = (bf16[136,768]{1,0:T(8,128)(2,1)S(1)}, bf16[136,768]{1,0:T(8,128)(2,1)S(1)}, u32[]{:S(2)}, u32[]{:S(2)}) collective-permute-start(bf16[136,768]{1,0:T(8,128)(2,1)S(1)} %add_convert_fusion), channel_id=1, source_target_pairs={{0,4},{1,5},{2,6},{3,7},{4,8},{5,9},{6,10},{7,11},{8,12},{9,13},{1... | collective-permute-start | bytes 626696 | tf_op jit(solution)/shard_map/ppermute | solution.py:31
